TPU v7x, 32 devices: a whole 2x2x4 slice. The times are simulated.
32 devices in a mesh: dp: 16 (over z, y, x), mp: 2 (over core).
Axes of the slice: x: 2, y: 2, z: 4, core: 2. Of those that a mesh axis runs over, the one named last changes fastest.
Arguments:
- log_rows: bfloat16 [98304, 256], P('dp'), may hold values from -6 to 6
- query_ids: int32 [98304], P('dp'), may hold values from 0 to 191, as said below
- doc_ranks: int32 [98304], P('dp'), may hold values from 0 to 511, as said below
- row_counts: int32 [16, 16], P('dp'), may hold values from 0 to 384, as said below
- list_lengths: int32 [192], P('dp'), may hold values from 64 to 512, as said below
- gains: float32 [192, 512], P('dp'), may hold values from 0.01 to 1
- weight_in: float32 [256, 4096], P(None, 'mp'), may hold values from -0.375 to 0.375
- bias_in: float32 [4096], P('mp'), may hold values from -3 to 3
- weight_out: float32 [4096], P('mp'), may hold values from -0.3 to 0.3
- moment_w: float32 [256, 4096], P(None, 'mp'), may hold values from -0.6 to 0.6
- second_w: float32 [256, 4096], P(None, 'mp'), may hold values from 0.05 to 2
- moment_b: float32 [4096], P('mp'), may hold values from -0.6 to 0.6
- second_b: float32 [4096], P('mp'), may hold values from 0.05 to 2
- moment_o: float32 [4096], P('mp'), may hold values from -0.6 to 0.6
- second_o: float32 [4096], P('mp'), may hold values from 0.05 to 2
Outputs:
- doc_lambdas: float32 [192, 512], P('dp')
- weight_in_next: float32 [256, 4096], P(None, 'mp')
- moment_w_next: float32 [256, 4096], P(None, 'mp')
- second_w_next: float32 [256, 4096], P(None, 'mp')
- bias_in_next: float32 [4096], P('mp')
- moment_b_next: float32 [4096], P('mp')
- second_b_next: float32 [4096], P('mp')
- weight_out_next: float32 [4096], P('mp')
- moment_o_next: float32 [4096], P('mp')
- second_o_next: float32 [4096], P('mp')
Inputs may be any that keep to these rules, and one draw needn't show every extreme that they name: row_counts[s, j] is at most 384; the live rows that all shards hold for owner j number list_lengths summed over owner j's queries j * 12 to j * 12 + 11; some owner receives 384 live rows from every shard. `query_ids`: A live row of the block for owner j belongs to one of owner j's queries; rows that are not live carry arbitrary ids. `doc_ranks`: the live rows of query q carry the ranks 0 to list_lengths[q] - 1, each once; rows that are not live carry arbitrary ranks. `list_lengths`: every owner has a list of 512 documents.
All inputs are finite; a program needn't handle non-finite values.
Results may differ from a plain program's by a relative error of at most 0.0049.
Values may be sent and summed in bfloat16 or wider, within the bound.
A program may use at most 192 MiB of HBM per device.

v0:
```python
import jax
import jax.numpy as jnp
from jax import lax
from jax.sharding import PartitionSpec as P

beta_one = 0.9
beta_two = 0.95
learn_rate = 0.001
adam_eps = 1e-08


def gelu_tanh(values):
    return jax.nn.gelu(values, approximate=True)


def owner_lambdas(score_rows, gain_rows, lengths):
    list_width = gain_rows.shape[1]
    positions = jnp.arange(list_width)
    discount = 1.0 / jnp.log2(2.0 + positions.astype(jnp.float32))
    keep_mask = (positions[None, :] < lengths[:, None]).astype(jnp.float32)

    def per_list(triple):
        row_score, row_gain, row_keep = triple
        delta_s = row_score[:, None] - row_score[None, :]
        delta_g = row_gain[:, None] - row_gain[None, :]
        weight = (
            jnp.abs(discount[:, None] - discount[None, :]) * row_keep[:, None] * row_keep[None, :]
        )
        pair_term = jnp.maximum(delta_g, 0.0) * jax.nn.sigmoid(-delta_s) - jnp.maximum(
            -delta_g, 0.0
        ) * jax.nn.sigmoid(delta_s)
        return -jnp.sum(weight * pair_term, axis=1)

    return lax.map(per_list, (score_rows, gain_rows, keep_mask))


def adam_step(weights, moment, second, gradient):
    moment_next = beta_one * moment + (1.0 - beta_one) * gradient
    second_next = beta_two * second + (1.0 - beta_two) * gradient * gradient
    weights_next = weights - learn_rate * moment_next / (jnp.sqrt(second_next) + adam_eps)
    return (weights_next, moment_next, second_next)


def per_device(
    log_rows,
    query_ids,
    doc_ranks,
    row_counts,
    list_lengths,
    gains,
    weight_in,
    bias_in,
    weight_out,
    moment_w,
    second_w,
    moment_b,
    second_b,
    moment_o,
    second_o,
):
    shard_count = lax.axis_size("dp")
    features = log_rows.shape[1]
    slot_count = log_rows.shape[0] // shard_count
    list_count, list_width = gains.shape
    owner_rows = list_count * list_width
    query_total = list_count * shard_count
    blocks = log_rows.reshape(shard_count, slot_count, features)
    is_live = jnp.arange(slot_count)[None, :] < row_counts.reshape(shard_count, 1)
    targets = jnp.where(
        is_live,
        query_ids.reshape(shard_count, slot_count) % list_count * list_width
        + doc_ranks.reshape(shard_count, slot_count),
        owner_rows,
    )
    w_low = weight_in.astype(jnp.bfloat16)
    arrived = lax.all_to_all(blocks, "dp", split_axis=0, concat_axis=0, tiled=True)
    arrived_slots = lax.all_to_all(targets, "dp", split_axis=0, concat_axis=0, tiled=True)
    used_rows = (
        jnp.zeros((owner_rows, features), jnp.bfloat16)
        .at[arrived_slots.reshape(-1)]
        .set(arrived.reshape(-1, features), mode="drop")
    )
    pre_act = jnp.dot(used_rows, w_low, preferred_element_type=jnp.float32) + bias_in
    hidden, gelu_back = jax.vjp(gelu_tanh, pre_act)
    scores = lax.psum(jnp.sum(hidden * weight_out, axis=1), "mp")
    lambdas = owner_lambdas(scores.reshape(list_count, list_width), gains, list_lengths)
    row_lambdas = lambdas.reshape(-1) / query_total
    grad_pre = gelu_back(row_lambdas[:, None] * weight_out)[0]
    grad_w = lax.dot_general(
        used_rows,
        grad_pre.astype(jnp.bfloat16),
        (((0,), (0,)), ((), ())),
        preferred_element_type=jnp.float32,
    )
    grad_b = jnp.sum(grad_pre, axis=0)
    grad_o = jnp.sum(row_lambdas[:, None] * hidden, axis=0)
    grad_w, grad_b, grad_o = lax.psum((grad_w, grad_b, grad_o), "dp")
    weight_next, moment_w_next, second_w_next = adam_step(weight_in, moment_w, second_w, grad_w)
    bias_next, moment_b_next, second_b_next = adam_step(bias_in, moment_b, second_b, grad_b)
    out_next, moment_o_next, second_o_next = adam_step(weight_out, moment_o, second_o, grad_o)
    return (
        lambdas,
        weight_next,
        moment_w_next,
        second_w_next,
        bias_next,
        moment_b_next,
        second_b_next,
        out_next,
        moment_o_next,
        second_o_next,
    )


def solution(mesh):
    placed = (
        P("dp", None),
        P("dp"),
        P("dp"),
        P("dp", None),
        P("dp"),
        P("dp", None),
        P(None, "mp"),
        P("mp"),
        P("mp"),
        P(None, "mp"),
        P(None, "mp"),
        P("mp"),
        P("mp"),
        P("mp"),
        P("mp"),
    )
    return jax.shard_map(
        per_device,
        mesh=mesh,
        in_specs=placed,
        out_specs=(
            P("dp", None),
            P(None, "mp"),
            P(None, "mp"),
            P(None, "mp"),
            P("mp"),
            P("mp"),
            P("mp"),
            P("mp"),
            P("mp"),
            P("mp"),
        ),
        check_vma=False,
    )
```

profile of v0, /device:TPU:0, one launch (start us, length us, event | category | flops | bytes accessed | tf_op | source)
XLA Modules:
  0.0 381.7 jit_solution(12026352199556250524)
XLA Ops:
  7.2 0.7 broadcast_remainder_fusion
  7.9 0.8 compare_select_fusion.1
  8.8 15.5 %all_to_all.11 = s32[16,1,384]{2,1,0:T(1,128)S(1)} all-to-all(s32[16,1,384]{2,1,0:T(1,128)S(1)} %compare_select_fusion.1), channel_id=1, replica_groups=mesh['dp'=16,'mp'=2] {'dp'}, dimensions={0} | all-to-all | bytes 49152 | tf_op jit(solution)/shard_map/all_to_all | solution.py:77
  24.2 3.7 all-to-all-start.1
  28.0 0.0 all-reduce.3.cloned.1.call-start
  28.1 0.7 fusion.29
  28.8 59.5 %all-to-all-done.1 = bf16[16,384,256]{2,1,0:T(8,128)(2,1)S(1)} async-done(((bf16[16,384,256]{2,1,0:T(8,128)(2,1)}), bf16[16,384,256]{2,1,0:T(8,128)(2,1)S(1)}, u32[]{:S(2)}, u32[]{:S(2)}) %all-to-all-start.1) | async-done | bytes 3145760 | tf_op jit(solution)/shard_map/all_to_all | solution.py:76
  88.3 1.7 copy-done
  89.9 27.8 %scatter_custom_fusion = bf16[6144,256]{1,0:T(8,128)(2,1)S(1)} fusion(s32[6144]{0:T(1024)S(1)} %bitcast.31, bf16[6144,256]{1,0:T(8,128)(2,1)} %bitcast.24, bf16[]{:T(256)} %constant.12.clone.1), kind=kCustom, calls=%fused_computation.43 | custom fusion | bytes 3146240 | tf_op jit(solution)/shard_map/scatter | solution.py:81
  117.8 0.0 copy-start.1
  117.8 0.0 copy-start.2
  117.8 26.4 %multiply_reduce_fusion.1 = (f32[6144]{0:T(1024)S(1)}, f32[6144,2048]{1,0:T(8,128)}) fusion(f32[2048]{0:T(1024)} %param.25, f32[2048]{0:T(1024)} %param.24, bf16[6144,256]{1,0:T(8,128)(2,1)S(1)} %scatter_custom_fusion, f32[256,2048]{1,0:T(8,128)} %param.23), kind=kOutput, calls=%fused_computation.35 | convolution fusion | flops 6581381120 | bytes 55615488 | tf_op jit(solution)/shard_map/dot_general | solution.py:83
  144.2 3.6 psum.28
  147.7 23.0 %while.11 = (s32[]{:T(128)}, f32[12,512]{1,0:T(8,128)S(1)}, f32[12,512]{1,0:T(8,128)S(1)}, f32[12,512]{1,0:T(8,128)}, f32[12,512]{1,0:T(8,128)S(1)}, /*index=5*/s32[]{:T(128)}, s32[]{:T(128)}) while((s32[]{:T(128)}, f32[12,512]{1,0:T(8,128)S(1)}, f32[12,512]{1,0:T(8,128)S(1)}, f32[12,512]{1,0:T(8,128)}, f32[12,512]{1,0:T(8,128)S(1)}, ...), condition=%wide.region_5.6_spmd.clone, body=%wide.region_3.5_spmd.clone.sunk | while | flops 4982786 | bytes 32865 | solution.py:34
  147.8 0.7 constant_dynamic-slice_fusion.5
  148.5 1.1 fusion.43
  149.6 0.1 dynamic_update_slice.6
  149.7 0.7 constant_dynamic-slice_fusion.5
  150.4 1.1 fusion.43
  151.5 0.1 dynamic_update_slice.6
  151.6 0.7 constant_dynamic-slice_fusion.5
  152.3 1.1 fusion.43
  153.4 0.1 dynamic_update_slice.6
  153.5 0.7 constant_dynamic-slice_fusion.5
  154.3 1.1 fusion.43
  155.3 0.1 dynamic_update_slice.6
  155.4 0.7 constant_dynamic-slice_fusion.5
  156.2 1.1 fusion.43
  157.2 0.1 dynamic_update_slice.6
  157.4 0.7 constant_dynamic-slice_fusion.5
  158.1 1.1 fusion.43
  159.2 0.1 dynamic_update_slice.6
  159.3 0.7 constant_dynamic-slice_fusion.5
  160.0 1.1 fusion.43
  161.1 0.1 dynamic_update_slice.6
  161.2 0.7 constant_dynamic-slice_fusion.5
  161.9 1.1 fusion.43
  163.0 0.1 dynamic_update_slice.6
  163.1 0.7 constant_dynamic-slice_fusion.5
  163.8 1.1 fusion.43
  164.9 0.1 dynamic_update_slice.6
  165.0 0.7 constant_dynamic-slice_fusion.5
  165.7 1.1 fusion.43
  166.8 0.1 dynamic_update_slice.6
  166.9 0.7 constant_dynamic-slice_fusion.5
  167.7 1.1 fusion.43
  168.7 0.1 dynamic_update_slice.6
  168.8 0.7 constant_dynamic-slice_fusion.5
  169.6 1.1 fusion.43
  170.6 0.1 dynamic_update_slice.6
  170.7 0.0 copy-start.3
  170.8 0.0 copy-done.1
  170.8 0.0 copy-done.2
  170.8 48.6 %fusion.36 = (f32[2048]{0:T(1024)S(1)}, bf16[6144,2048]{1,0:T(8,128)(2,1)}, f32[2048]{0:T(1024)S(1)}) fusion(f32[6144,2048]{1,0:T(8,128)} %get-tuple-element.82, f32[2048]{0:T(1024)S(1)} %copy-done.2, f32[2048]{0:T(1024)S(1)} %copy-done.1, f32[6144]{0:T(1024)S(1)} %div.33), kind=kLoop, calls=%fused_computation.64 | loop fusion | flops 327151616 | bytes 75554816 | tf_op jit(solution)/shard_map/reduce_sum | solution.py:95
  219.4 0.0 copy-start.4
  219.4 0.0 copy-start.5
  219.4 0.0 copy-start.6
  219.4 0.0 copy-start.7
  219.5 12.9 %fusion.22 = f32[256,2048]{1,0:T(8,128)} fusion(bf16[6144,256]{1,0:T(8,128)(2,1)S(1)} %scatter_custom_fusion, bf16[6144,2048]{1,0:T(8,128)(2,1)} %get-tuple-element.74), kind=kOutput, calls=%fused_computation.37 | convolution fusion | flops 6442450944 | bytes 30408704 | tf_op jit(solution)/shard_map/dot_general | solution.py:89
  232.4 0.0 all-reduce.3.cloned.1.call-update
  232.4 84.9 %all-reduce = (f32[2048]{0:T(1024)S(1)}, f32[2048]{0:T(1024)S(1)}) all-reduce(f32[2048]{0:T(1024)S(1)} %get-tuple-element.73, f32[2048]{0:T(1024)S(1)} %get-tuple-element.80), channel_id=1, replica_groups=mesh['dp'=16,'mp'=2] {'dp'}, use_global_device_ids=true, to_apply=%region_8.9 | all-reduce | flops 4096 | bytes 32768 | tf_op jit(solution)/shard_map/psum | solution.py:97
  317.4 0.6 divide_subtract_fusion.1
  318.0 49.5 %all-reduce.3.cloned.1.call-done = f32[256,2048]{1,0:T(8,128)} async-done(((f32[256,2048]{1,0:T(8,128)}), f32[256,2048]{1,0:T(8,128)}) %all-reduce.3.cloned.1.call-update) | async-done | bytes 2097168 | tf_op jit(solution)/shard_map/psum | solution.py:97
  367.5 7.4 %divide_subtract_fusion = (f32[256,2048]{1,0:T(8,128)}, f32[256,2048]{1,0:T(8,128)}, f32[256,2048]{1,0:T(8,128)}) fusion(f32[256,2048]{1,0:T(8,128)} %param.23, f32[256,2048]{1,0:T(8,128)} %all-reduce.3.cloned.1.call-done, f32[256,2048]{1,0:T(8,128)} %param.26, f32[256,2048]{1,0:T(8,128)} %param.27), kind=kLoop, calls=%fused_computation.41 | loop fusion | flops 5767168 | bytes 14680064 | tf_op jit(solution)/shard_map/sub | solution.py:40
  (47 shorter events, 0.3 us)
Async XLA Ops:
  24.2 64.0 %all-to-all-start.1 = ((bf16[16,384,256]{2,1,0:T(8,128)(2,1)}), bf16[16,384,256]{2,1,0:T(8,128)(2,1)S(1)}, u32[]{:S(2)}, u32[]{:S(2)}) async-start(bf16[16,384,256]{2,1,0:T(8,128)(2,1)} %bitcast.23), calls=%async_computation.1 | async-start | bytes 6291456 | tf_op jit(solution)/shard_map/all_to_all | solution.py:76
  28.0 339.5 %all-reduce.3.cloned.1.call-start = ((), (), s32[]{:S(2)}) async-start(), calls=%async_computation.2 | async-start | bytes 4194304 | tf_op jit(solution)/shard_map/psum | solution.py:97
  88.3 1.7 copy-start
  117.8 53.0 %copy-start.1 = (f32[2048]{0:T(1024)S(1)}, f32[2048]{0:T(1024)}, u32[]{:S(2)}) copy-start(f32[2048]{0:T(1024)} %param.25) | copy-start | bytes 24580
  117.8 53.0 %copy-start.2 = (f32[2048]{0:T(1024)S(1)}, f32[2048]{0:T(1024)}, u32[]{:S(2)}) copy-start(f32[2048]{0:T(1024)} %param.24) | copy-start | bytes 24580
  170.7 48.7 %copy-start.3 = (f32[12,512]{1,0:T(8,128)}, f32[12,512]{1,0:T(8,128)S(1)}, u32[]{:S(2)}) copy-start(f32[12,512]{1,0:T(8,128)S(1)} %get-tuple-element.32) | copy-start | bytes 73732
  219.4 98.0 %copy-start.4 = (f32[2048]{0:T(1024)S(1)}, f32[2048]{0:T(1024)}, u32[]{:S(2)}) copy-start(f32[2048]{0:T(1024)} %param.30) | copy-start | bytes 24580
  219.4 97.9 %copy-start.5 = (f32[2048]{0:T(1024)S(1)}, f32[2048]{0:T(1024)}, u32[]{:S(2)}) copy-start(f32[2048]{0:T(1024)} %param.31) | copy-start | bytes 24580
  219.4 97.9 %copy-start.6 = (f32[2048]{0:T(1024)S(1)}, f32[2048]{0:T(1024)}, u32[]{:S(2)}) copy-start(f32[2048]{0:T(1024)} %param.29) | copy-start | bytes 24580
  219.4 97.9 %copy-start.7 = (f32[2048]{0:T(1024)S(1)}, f32[2048]{0:T(1024)}, u32[]{:S(2)}) copy-start(f32[2048]{0:T(1024)} %param.28) | copy-start | bytes 24580
Sparse Core Ops, SparseCore 0:
  232.5 134.8 all-reduce.2
where the time goes:
time: 383 us; the launch traced here: 382 us
  waiting for transfers between devices  109 us (28%)
  blocking collectives  104 us (27%)
  other arithmetic  71.8 us (19%)
  matrix products  39.3 us (10%)
  local copies, waits for them, and re-layouts  39.2 us (10%)
  between operations  14.2 us (4%)
    psum x1, blocking collectives, per_device(): grad_w, grad_b, grad_o = lax.psum((grad_w, grad_b, grad_o), 'dp')  84.9 us
    all_to_all x1, waiting for transfers between devices, per_device(): lax.all_to_all(blocks, 'dp', split_axis=0, concat_axis=0, tiled=True)  59.5 us
    psum x1, waiting for transfers between devices, per_device(): grad_w, grad_b, grad_o = lax.psum((grad_w, grad_b, grad_o), 'dp')  49.5 us
    reduce_sum x1, other arithmetic, per_device(): grad_b = jnp.sum(grad_pre, axis=0)  48.6 us
    scatter x1, local copies, waits for them, and re-layouts, per_device(): used_rows = jnp.zeros((owner_rows, features), jnp.bfloat16).at[arrived_sl...  27.8 us
    dot_general x1, matrix products, per_device(): jnp.dot(used_rows, w_low, preferred_element_type=jnp.float32) + bias_in  26.4 us
    all_to_all x1, blocking collectives, per_device(): lax.all_to_all(targets, 'dp', split_axis=0, concat_axis=0, tiled=True)  15.5 us
    dot_general x1, matrix products, per_device(): lax.dot_general(used_rows, grad_pre.astype(jnp.bfloat16), (((0,), (0,)),...  12.9 us
  transfers between devices with their start and end apart: 2, of which 2 were waited for; matrix products, arithmetic and copies ran while one was open for 0% of the time, Pallas kernels for 0%

commit v1 on v0

--- a/solution.py
+++ b/solution.py
@@ -7,6 +7,22 @@
 beta_two = 0.95
 learn_rate = 0.001
 adam_eps = 1e-08
+
+
+def pairwise_exchange(value, axis, split, join):
+    ways, here = (lax.axis_size(axis), lax.axis_index(axis))
+    width = value.shape[split] // ways
+    shape = list(value.shape)
+    shape[split] = width
+    height = shape[join]
+    shape[join] = height * ways
+    full = jnp.zeros(shape, value.dtype)
+    for mask in range(ways):
+        part = lax.dynamic_slice_in_dim(value, (here ^ mask) * width, width, axis=split)
+        if mask:
+            part = lax.ppermute(part, axis, [(d, d ^ mask) for d in range(ways)])
+        full = lax.dynamic_update_slice_in_dim(full, part, (here ^ mask) * height, axis=join)
+    return full
 
 
 def gelu_tanh(values):
@@ -73,7 +89,7 @@
         owner_rows,
     )
     w_low = weight_in.astype(jnp.bfloat16)
-    arrived = lax.all_to_all(blocks, "dp", split_axis=0, concat_axis=0, tiled=True)
+    arrived = pairwise_exchange(blocks, "dp", 0, 0)
     arrived_slots = lax.all_to_all(targets, "dp", split_axis=0, concat_axis=0, tiled=True)
     used_rows = (
         jnp.zeros((owner_rows, features), jnp.bfloat16)

time: 383 us -> 399 us (1.042)
  starting transfers between devices: 3.78 us -> 33.3 us
  blocking collectives: 104 us -> 79.5 us
  local copies, waits for them, and re-layouts: 39.2 us -> 60 us
  waiting for transfers between devices: 109 us -> 96.1 us
    all_to_all x1, waiting for transfers between devices: 59.5 us -> 0.01 us  [per_device(): lax.all_to_all(targets, 'dp', split_axis=0, concat_axis=0, tiled=True)]
    ppermute x0 -> x15, waiting for transfers between devices: none -> 46.2 us  [pairwise_exchange(): part = lax.ppermute(part, axis, [(d, d ^ mask) for d in range(ways)])]
    ppermute x0 -> x15, starting transfers between devices: none -> 24.9 us  [pairwise_exchange(): part = lax.ppermute(part, axis, [(d, d ^ mask) for d in range(ways)])]
    all_to_all x1 -> x0, blocking collectives: 15.5 us -> none  [per_device(): lax.all_to_all(targets, 'dp', split_axis=0, concat_axis=0, tiled=True)]
    dynamic_update_slice x0 -> x15, local copies, waits for them, and re-layouts: none -> 10.4 us  [pairwise_exchange(): lax.dynamic_update_slice_in_dim(full, part, (here ^ mask) * height, axis=...]
    psum x1, blocking collectives: 84.9 us -> 75.9 us  [per_device(): grad_w, grad_b, grad_o = lax.psum((grad_w, grad_b, grad_o), 'dp')]
    dynamic_slice x24, local copies, waits for them, and re-layouts: 8.89 us -> 17.5 us  [owner_lambdas(): return lax.map(per_list, (score_rows, gain_rows, keep_mask))]
    all_to_all x1, starting transfers between devices: 3.74 us -> 8.36 us  [per_device(): lax.all_to_all(targets, 'dp', split_axis=0, concat_axis=0, tiled=True)]
  transfers between devices with their start and end apart: 2 -> 17, of which waited for: 2 -> 10; matrix products, arithmetic and copies ran while one was open for 0% -> 4% of each run, Pallas kernels for 0% -> 0%
where the time goes in v1:
time: 399 us; the launch traced here: 396 us
  waiting for transfers between devices  96.1 us (24%)
  blocking collectives  79.5 us (20%)
  other arithmetic  73.1 us (18%)
  local copies, waits for them, and re-layouts  60 us (15%)
  matrix products  39.4 us (10%)
  starting transfers between devices  33.3 us (8%)
  between operations  14.3 us (4%)
    psum x1, blocking collectives, per_device(): grad_w, grad_b, grad_o = lax.psum((grad_w, grad_b, grad_o), 'dp')  75.9 us
    psum x1, waiting for transfers between devices, per_device(): grad_w, grad_b, grad_o = lax.psum((grad_w, grad_b, grad_o), 'dp')  49.9 us
    reduce_sum x1, other arithmetic, per_device(): grad_b = jnp.sum(grad_pre, axis=0)  48.7 us
    ppermute x15, waiting for transfers between devices, pairwise_exchange(): part = lax.ppermute(part, axis, [(d, d ^ mask) for d in range(ways)])  46.2 us
    scatter x1, local copies, waits for them, and re-layouts, per_device(): used_rows = jnp.zeros((owner_rows, features), jnp.bfloat16).at[arrived_sl...  27.8 us
    dot_general x1, matrix products, per_device(): jnp.dot(used_rows, w_low, preferred_element_type=jnp.float32) + bias_in  26.4 us
    ppermute x15, starting transfers between devices, pairwise_exchange(): part = lax.ppermute(part, axis, [(d, d ^ mask) for d in range(ways)])  24.9 us
    dynamic_slice x24, local copies, waits for them, and re-layouts, owner_lambdas(): return lax.map(per_list, (score_rows, gain_rows, keep_mask))  17.5 us
  transfers between devices with their start and end apart: 17, of which 10 were waited for; matrix products, arithmetic and copies ran while one was open for 4% of the time, Pallas kernels for 0%

profile of v1, /device:TPU:0, one launch (start us, length us, event | category | flops | bytes accessed | tf_op | source)
XLA Modules:
  0.0 396.1 jit_solution(1277744171547035305)
XLA Ops:
  7.2 0.9 broadcast_remainder_fusion
  8.1 1.5 compare_select_fusion.1
  9.6 8.4 %all-to-all-start = ((s32[16,1,384]{2,1,0:T(1,128)}), s32[16,1,384]{2,1,0:T(1,128)}, u32[]{:S(2)}, u32[]{:S(2)}) async-start(s32[16,1,384]{2,1,0:T(1,128)} %compare_select_fusion.1), calls=%async_computation | async-start | bytes 49152 | tf_op jit(solution)/shard_map/all_to_all | solution.py:93
  18.4 1.5 constant_dynamic-slice_fusion.3
  19.9 1.6 copy-done.1
  21.6 5.5 %collective-permute-start.14 = (bf16[1,384,256]{2,1,0:T(8,128)(2,1)S(1)}, bf16[1,384,256]{2,1,0:T(8,128)(2,1)S(1)}, u32[]{:S(2)}, u32[]{:S(2)}) collective-permute-start(bf16[1,384,256]{2,1,0:T(8,128)(2,1)S(1)} %get-tuple-element.81), channel_id=1, source_target_pairs={{0,30},{2,28},{4,26},{6,24},{8,22},{10,20},{12,18},{14,16},{16,14}... | collective-permute-start | bytes 589832 | tf_op jit(solution)/shard_map/ppermute | solution.py:23
  27.6 3.3 collective-permute-start.12
  30.9 1.5 collective-permute-start.1
  32.3 1.5 collective-permute-start
  34.5 1.4 compare_select_fusion
  35.8 7.3 %collective-permute-done = bf16[1,384,256]{2,1,0:T(8,128)(2,1)S(1)} collective-permute-done((bf16[1,384,256]{2,1,0:T(8,128)(2,1)}, bf16[1,384,256]{2,1,0:T(8,128)(2,1)S(1)}, u32[]{:S(2)}, u32[]{:S(2)}) %collective-permute-start) | collective-permute-done | bytes 196640 | tf_op jit(solution)/shard_map/ppermute | solution.py:23
  43.1 1.4 collective-permute-start.2
  45.9 6.2 %collective-permute-done.2 = bf16[1,384,256]{2,1,0:T(8,128)(2,1)S(1)} collective-permute-done((bf16[1,384,256]{2,1,0:T(8,128)(2,1)}, bf16[1,384,256]{2,1,0:T(8,128)(2,1)S(1)}, u32[]{:S(2)}, u32[]{:S(2)}) %collective-permute-start.2) | collective-permute-done | bytes 196640 | tf_op jit(solution)/shard_map/ppermute | solution.py:23
  52.1 3.4 collective-permute-start.4
  56.9 4.8 %collective-permute-done.4 = bf16[1,384,256]{2,1,0:T(8,128)(2,1)S(1)} collective-permute-done((bf16[1,384,256]{2,1,0:T(8,128)(2,1)}, bf16[1,384,256]{2,1,0:T(8,128)(2,1)S(1)}, u32[]{:S(2)}, u32[]{:S(2)}) %collective-permute-start.4) | collective-permute-done | bytes 196640 | tf_op jit(solution)/shard_map/ppermute | solution.py:23
  62.3 1.6 collective-permute-done.5
  64.6 6.4 %collective-permute-done.6 = bf16[1,384,256]{2,1,0:T(8,128)(2,1)S(1)} collective-permute-done((bf16[1,384,256]{2,1,0:T(8,128)(2,1)}, bf16[1,384,256]{2,1,0:T(8,128)(2,1)S(1)}, u32[]{:S(2)}, u32[]{:S(2)}) %collective-permute-start.6) | collective-permute-done | bytes 196640 | tf_op jit(solution)/shard_map/ppermute | solution.py:23
  71.7 5.4 %collective-permute-done.7 = bf16[1,384,256]{2,1,0:T(8,128)(2,1)S(1)} collective-permute-done((bf16[1,384,256]{2,1,0:T(8,128)(2,1)}, bf16[1,384,256]{2,1,0:T(8,128)(2,1)S(1)}, u32[]{:S(2)}, u32[]{:S(2)}) %collective-permute-start.7) | collective-permute-done | bytes 196640 | tf_op jit(solution)/shard_map/ppermute | solution.py:23
  77.1 3.0 collective-permute-start.9
  80.8 6.8 %collective-permute-done.8 = bf16[1,384,256]{2,1,0:T(8,128)(2,1)S(1)} collective-permute-done((bf16[1,384,256]{2,1,0:T(8,128)(2,1)}, bf16[1,384,256]{2,1,0:T(8,128)(2,1)S(1)}, u32[]{:S(2)}, u32[]{:S(2)}) %collective-permute-start.8) | collective-permute-done | bytes 196640 | tf_op jit(solution)/shard_map/ppermute | solution.py:23
  88.4 5.3 %collective-permute-done.9 = bf16[1,384,256]{2,1,0:T(8,128)(2,1)S(1)} collective-permute-done((bf16[1,384,256]{2,1,0:T(8,128)(2,1)}, bf16[1,384,256]{2,1,0:T(8,128)(2,1)S(1)}, u32[]{:S(2)}, u32[]{:S(2)}) %collective-permute-start.9) | collective-permute-done | bytes 196640 | tf_op jit(solution)/shard_map/ppermute | solution.py:23
  93.7 4.9 %collective-permute-start.11 = (bf16[1,384,256]{2,1,0:T(8,128)(2,1)S(1)}, bf16[1,384,256]{2,1,0:T(8,128)(2,1)S(1)}, u32[]{:S(2)}, u32[]{:S(2)}) collective-permute-start(bf16[1,384,256]{2,1,0:T(8,128)(2,1)S(1)} %copy-done.3), channel_id=1, source_target_pairs={{0,24},{2,26},{4,28},{6,30},{8,16},{10,18},{12,20},{14,22},{16,8},... | collective-permute-start | bytes 589832 | tf_op jit(solution)/shard_map/ppermute | solution.py:23
  100.0 2.4 collective-permute-done.11
  105.2 27.8 %scatter_custom_fusion = bf16[6144,256]{1,0:T(8,128)(2,1)S(1)} fusion(s32[6144]{0:T(1024)} %bitcast.30, bf16[6144,256]{1,0:T(8,128)(2,1)} %bitcast.24, bf16[]{:T(256)} %constant.50.clone.1), kind=kCustom, calls=%fused_computation.43 | custom fusion | bytes 3146240 | tf_op jit(solution)/shard_map/scatter | solution.py:97
  133.0 26.4 %multiply_reduce_fusion.1 = (f32[6144]{0:T(1024)S(1)}, f32[6144,2048]{1,0:T(8,128)}) fusion(f32[2048]{0:T(1024)S(1)} %copy-done.5, f32[2048]{0:T(1024)S(1)} %copy-done.6, bf16[6144,256]{1,0:T(8,128)(2,1)S(1)} %scatter_custom_fusion, f32[256,2048]{1,0:T(8,128)} %param.23), kind=kOutput, calls=%fused_computation.35 | convolution fusion | flops 6581381120 | bytes 55615488 | tf_op jit(solution)/shard_map/dot_general | solution.py:99
  159.4 3.6 psum.28
  163.0 31.5 %while.11 = (s32[]{:T(128)}, f32[12,512]{1,0:T(8,128)S(1)}, f32[12,512]{1,0:T(8,128)}, f32[12,512]{1,0:T(8,128)}, f32[12,512]{1,0:T(8,128)S(1)}, /*index=5*/s32[]{:T(128)}, s32[]{:T(128)}) while((s32[]{:T(128)}, f32[12,512]{1,0:T(8,128)S(1)}, f32[12,512]{1,0:T(8,128)}, f32[12,512]{1,0:T(8,128)}, f32[12,512]{1,0:T(8,128)S(1)}, ...), condition=%wide.region_5.6_spmd.clone, body=%wide.region_3.5_spmd.clone.sunk | while | flops 4982786 | bytes 32865 | solution.py:50
  163.0 0.7 constant_dynamic-slice_fusion.21
  163.8 0.7 constant_dynamic-slice_fusion.20
  164.5 1.1 fusion.43
  165.6 0.7 constant_dynamic-slice_fusion.21
  166.4 0.7 constant_dynamic-slice_fusion.20
  167.1 1.1 fusion.43
  168.3 0.7 constant_dynamic-slice_fusion.21
  169.0 0.7 constant_dynamic-slice_fusion.20
  169.7 1.1 fusion.43
  170.9 0.7 constant_dynamic-slice_fusion.21
  171.6 0.7 constant_dynamic-slice_fusion.20
  172.3 1.1 fusion.43
  173.5 0.7 constant_dynamic-slice_fusion.21
  174.2 0.7 constant_dynamic-slice_fusion.20
  175.0 1.1 fusion.43
  176.1 0.7 constant_dynamic-slice_fusion.21
  176.9 0.7 constant_dynamic-slice_fusion.20
  177.6 1.1 fusion.43
  178.7 0.7 constant_dynamic-slice_fusion.21
  179.5 0.7 constant_dynamic-slice_fusion.20
  180.2 1.1 fusion.43
  182.1 0.7 constant_dynamic-slice_fusion.20
  182.8 1.1 fusion.43
  184.7 0.7 constant_dynamic-slice_fusion.20
  185.5 1.1 fusion.43
  187.3 0.7 constant_dynamic-slice_fusion.20
  188.1 1.1 fusion.43
  190.0 0.7 constant_dynamic-slice_fusion.20
  190.7 1.1 fusion.43
  191.8 0.7 constant_dynamic-slice_fusion.21
  192.6 0.7 constant_dynamic-slice_fusion.20
  193.3 1.1 fusion.43
  194.5 48.7 %fusion.36 = (f32[2048]{0:T(1024)S(1)}, bf16[6144,2048]{1,0:T(8,128)(2,1)}, f32[2048]{0:T(1024)S(1)}) fusion(f32[6144,2048]{1,0:T(8,128)} %get-tuple-element.98, f32[2048]{0:T(1024)S(1)} %copy-done.6, f32[2048]{0:T(1024)S(1)} %copy-done.5, f32[6144]{0:T(1024)S(1)} %div.33), kind=kLoop, calls=%fused_computation.95 | loop fusion | flops 327151616 | bytes 75554816 | tf_op jit(solution)/shard_map/reduce_sum | solution.py:111
  243.2 12.9 %fusion.22 = f32[256,2048]{1,0:T(8,128)} fusion(bf16[6144,256]{1,0:T(8,128)(2,1)S(1)} %scatter_custom_fusion, bf16[6144,2048]{1,0:T(8,128)(2,1)} %get-tuple-element.74), kind=kOutput, calls=%fused_computation.37 | convolution fusion | flops 6442450944 | bytes 30408704 | tf_op jit(solution)/shard_map/dot_general | solution.py:105
  256.2 75.9 %all-reduce = (f32[2048]{0:T(1024)S(1)}, f32[2048]{0:T(1024)S(1)}) all-reduce(f32[2048]{0:T(1024)S(1)} %get-tuple-element.73, f32[2048]{0:T(1024)S(1)} %get-tuple-element.80), channel_id=1, replica_groups=mesh['dp'=16,'mp'=2] {'dp'}, use_global_device_ids=true, to_apply=%region_8.9 | all-reduce | flops 4096 | bytes 32768 | tf_op jit(solution)/shard_map/psum | solution.py:113
  332.8 49.9 %all-reduce.3.cloned.1.call-done = f32[256,2048]{1,0:T(8,128)} async-done(((f32[256,2048]{1,0:T(8,128)}), f32[256,2048]{1,0:T(8,128)}) %all-reduce.3.cloned.1.call-update) | async-done | bytes 2097168 | tf_op jit(solution)/shard_map/psum | solution.py:113
  382.6 6.6 %divide_subtract_fusion = (f32[256,2048]{1,0:T(8,128)}, f32[256,2048]{1,0:T(8,128)}, f32[256,2048]{1,0:T(8,128)}) fusion(f32[256,2048]{1,0:T(8,128)S(1)} %copy-done.2, f32[256,2048]{1,0:T(8,128)} %all-reduce.3.cloned.1.call-done, f32[256,2048]{1,0:T(8,128)} %param.26, f32[256,2048]{1,0:T(8,128)} %param.27), kind=kLoop, calls=%fused_computation.41 | loop fusion | flops 5767168 | bytes 14680064 | tf_op jit(solution)/shard_map/sub | solution.py:56
  (105 shorter events, 16.5 us)
Async XLA Ops:
  7.2 11.2 %copy-start = (bf16[6144,256]{1,0:T(8,128)(2,1)S(1)}, bf16[6144,256]{1,0:T(8,128)(2,1)}, u32[]{:S(2)}) copy-start(bf16[6144,256]{1,0:T(8,128)(2,1)} %param.17) | copy-start | bytes 9437188
  9.6 24.9 %all-to-all-start = ((s32[16,1,384]{2,1,0:T(1,128)}), s32[16,1,384]{2,1,0:T(1,128)}, u32[]{:S(2)}, u32[]{:S(2)}) async-start(s32[16,1,384]{2,1,0:T(1,128)} %compare_select_fusion.1), calls=%async_computation | async-start | bytes 49152 | tf_op jit(solution)/shard_map/all_to_all | solution.py:93
  17.9 364.7 %all-reduce.3.cloned.1.call-start = ((), (), s32[]{:S(2)}) async-start(), calls=%async_computation.1 | async-start | bytes 4194304 | tf_op jit(solution)/shard_map/psum | solution.py:113
  18.4 15.4 %copy-start.13 = (s32[12]{0:T(128)S(1)}, s32[12]{0:T(128)}, u32[]{:S(2)}) copy-start(s32[12]{0:T(128)} %param.21) | copy-start | bytes 148
  19.9 1.6 copy-start.1
  21.6 66.1 %copy-start.4 = (bf16[1,384,256]{2,1,0:T(8,128)(2,1)S(1)}, bf16[1,384,256]{2,1,0:T(8,128)(2,1)}, u32[]{:S(2)}) copy-start(bf16[1,384,256]{2,1,0:T(8,128)(2,1)} %get-tuple-element.85) | copy-start | bytes 589828
  21.6 72.2 %copy-start.3 = (bf16[1,384,256]{2,1,0:T(8,128)(2,1)S(1)}, bf16[1,384,256]{2,1,0:T(8,128)(2,1)}, u32[]{:S(2)}) copy-start(bf16[1,384,256]{2,1,0:T(8,128)(2,1)} %get-tuple-element.84) | copy-start | bytes 589828
  21.6 82.9 %collective-permute-start.14 = (bf16[1,384,256]{2,1,0:T(8,128)(2,1)S(1)}, bf16[1,384,256]{2,1,0:T(8,128)(2,1)S(1)}, u32[]{:S(2)}, u32[]{:S(2)}) collective-permute-start(bf16[1,384,256]{2,1,0:T(8,128)(2,1)S(1)} %get-tuple-element.81), channel_id=1, source_target_pairs={{0,30},{2,28},{4,26},{6,24},{8,22},{10,20},{12,18},{14,16},{16,14}... | collective-permute-start | bytes 589832 | tf_op jit(solution)/shard_map/ppermute | solution.py:23
  27.0 76.7 %collective-permute-start.13 = (bf16[1,384,256]{2,1,0:T(8,128)(2,1)S(1)}, bf16[1,384,256]{2,1,0:T(8,128)(2,1)S(1)}, u32[]{:S(2)}, u32[]{:S(2)}) collective-permute-start(bf16[1,384,256]{2,1,0:T(8,128)(2,1)S(1)} %get-tuple-element.82), channel_id=1, source_target_pairs={{0,28},{2,30},{4,24},{6,26},{8,20},{10,22},{12,16},{14,18},{16,12}... | collective-permute-start | bytes 589832 | tf_op jit(solution)/shard_map/ppermute | solution.py:23
  27.6 75.5 %collective-permute-start.12 = (bf16[1,384,256]{2,1,0:T(8,128)(2,1)}, bf16[1,384,256]{2,1,0:T(8,128)(2,1)S(1)}, u32[]{:S(2)}, u32[]{:S(2)}) collective-permute-start(bf16[1,384,256]{2,1,0:T(8,128)(2,1)} %get-tuple-element.83), channel_id=1, source_target_pairs={{0,26},{2,24},{4,30},{6,28},{8,18},{10,16},{12,22},{14,20},{16,10}... | collective-permute-start | bytes 589832 | tf_op jit(solution)/shard_map/ppermute | solution.py:23
  30.9 14.3 %collective-permute-start.1 = (bf16[1,384,256]{2,1,0:T(8,128)(2,1)}, bf16[1,384,256]{2,1,0:T(8,128)(2,1)S(1)}, u32[]{:S(2)}, u32[]{:S(2)}) collective-permute-start(bf16[1,384,256]{2,1,0:T(8,128)(2,1)} %get-tuple-element.94), channel_id=1, source_target_pairs={{0,4},{2,6},{4,0},{6,2},{8,12},{10,14},{12,8},{14,10},{16,20},{18,... | collective-permute-start | bytes 589832 | tf_op jit(solution)/shard_map/ppermute | solution.py:23
  32.3 10.8 %collective-permute-start = (bf16[1,384,256]{2,1,0:T(8,128)(2,1)}, bf16[1,384,256]{2,1,0:T(8,128)(2,1)S(1)}, u32[]{:S(2)}, u32[]{:S(2)}) collective-permute-start(bf16[1,384,256]{2,1,0:T(8,128)(2,1)} %get-tuple-element.95), channel_id=1, source_target_pairs={{0,2},{2,0},{4,6},{6,4},{8,10},{10,8},{12,14},{14,12},{16,18},{18,... | collective-permute-start | bytes 589832 | tf_op jit(solution)/shard_map/ppermute | solution.py:23
  43.1 9.0 %collective-permute-start.2 = (bf16[1,384,256]{2,1,0:T(8,128)(2,1)}, bf16[1,384,256]{2,1,0:T(8,128)(2,1)S(1)}, u32[]{:S(2)}, u32[]{:S(2)}) collective-permute-start(bf16[1,384,256]{2,1,0:T(8,128)(2,1)} %get-tuple-element.93), channel_id=1, source_target_pairs={{0,6},{2,4},{4,2},{6,0},{8,14},{10,12},{12,10},{14,8},{16,22},{18,... | collective-permute-start | bytes 589832 | tf_op jit(solution)/shard_map/ppermute | solution.py:23
  45.2 11.0 %collective-permute-start.3 = (bf16[1,384,256]{2,1,0:T(8,128)(2,1)}, bf16[1,384,256]{2,1,0:T(8,128)(2,1)S(1)}, u32[]{:S(2)}, u32[]{:S(2)}) collective-permute-start(bf16[1,384,256]{2,1,0:T(8,128)(2,1)} %get-tuple-element.92), channel_id=1, source_target_pairs={{0,8},{2,10},{4,12},{6,14},{8,0},{10,2},{12,4},{14,6},{16,24},{18,... | collective-permute-start | bytes 589832 | tf_op jit(solution)/shard_map/ppermute | solution.py:23
  52.1 9.5 %collective-permute-start.4 = (bf16[1,384,256]{2,1,0:T(8,128)(2,1)}, bf16[1,384,256]{2,1,0:T(8,128)(2,1)S(1)}, u32[]{:S(2)}, u32[]{:S(2)}) collective-permute-start(bf16[1,384,256]{2,1,0:T(8,128)(2,1)} %get-tuple-element.91), channel_id=1, source_target_pairs={{0,10},{2,8},{4,14},{6,12},{8,2},{10,0},{12,6},{14,4},{16,26},{18,... | collective-permute-start | bytes 589832 | tf_op jit(solution)/shard_map/ppermute | solution.py:23
  56.2 7.7 %collective-permute-start.5 = (bf16[1,384,256]{2,1,0:T(8,128)(2,1)}, bf16[1,384,256]{2,1,0:T(8,128)(2,1)S(1)}, u32[]{:S(2)}, u32[]{:S(2)}) collective-permute-start(bf16[1,384,256]{2,1,0:T(8,128)(2,1)} %get-tuple-element.90), channel_id=1, source_target_pairs={{0,12},{2,14},{4,8},{6,10},{8,4},{10,6},{12,0},{14,2},{16,28},{18,... | collective-permute-start | bytes 589832 | tf_op jit(solution)/shard_map/ppermute | solution.py:23
  61.6 9.3 %collective-permute-start.6 = (bf16[1,384,256]{2,1,0:T(8,128)(2,1)}, bf16[1,384,256]{2,1,0:T(8,128)(2,1)S(1)}, u32[]{:S(2)}, u32[]{:S(2)}) collective-permute-start(bf16[1,384,256]{2,1,0:T(8,128)(2,1)} %get-tuple-element.89), channel_id=1, source_target_pairs={{0,14},{2,12},{4,10},{6,8},{8,6},{10,4},{12,2},{14,0},{16,30},{18,... | collective-permute-start | bytes 589832 | tf_op jit(solution)/shard_map/ppermute | solution.py:23
  63.9 13.2 %collective-permute-start.7 = (bf16[1,384,256]{2,1,0:T(8,128)(2,1)}, bf16[1,384,256]{2,1,0:T(8,128)(2,1)S(1)}, u32[]{:S(2)}, u32[]{:S(2)}) collective-permute-start(bf16[1,384,256]{2,1,0:T(8,128)(2,1)} %get-tuple-element.88), channel_id=1, source_target_pairs={{0,16},{2,18},{4,20},{6,22},{8,24},{10,26},{12,28},{14,30},{16,0},... | collective-permute-start | bytes 589832 | tf_op jit(solution)/shard_map/ppermute | solution.py:23
  71.0 16.7 %collective-permute-start.8 = (bf16[1,384,256]{2,1,0:T(8,128)(2,1)}, bf16[1,384,256]{2,1,0:T(8,128)(2,1)S(1)}, u32[]{:S(2)}, u32[]{:S(2)}) collective-permute-start(bf16[1,384,256]{2,1,0:T(8,128)(2,1)} %get-tuple-element.87), channel_id=1, source_target_pairs={{0,18},{2,16},{4,22},{6,20},{8,26},{10,24},{12,30},{14,28},{16,2},... | collective-permute-start | bytes 589832 | tf_op jit(solution)/shard_map/ppermute | solution.py:23
  77.1 55.9 %copy-start.5 = (f32[2048]{0:T(1024)S(1)}, f32[2048]{0:T(1024)}, u32[]{:S(2)}) copy-start(f32[2048]{0:T(1024)} %param.25) | copy-start | bytes 24580
  77.1 55.9 %copy-start.6 = (f32[2048]{0:T(1024)S(1)}, f32[2048]{0:T(1024)}, u32[]{:S(2)}) copy-start(f32[2048]{0:T(1024)} %param.24) | copy-start | bytes 24580
  77.1 16.6 %collective-permute-start.9 = (bf16[1,384,256]{2,1,0:T(8,128)(2,1)}, bf16[1,384,256]{2,1,0:T(8,128)(2,1)S(1)}, u32[]{:S(2)}, u32[]{:S(2)}) collective-permute-start(bf16[1,384,256]{2,1,0:T(8,128)(2,1)} %get-tuple-element.86), channel_id=1, source_target_pairs={{0,20},{2,22},{4,16},{6,18},{8,28},{10,30},{12,24},{14,26},{16,4},... | collective-permute-start | bytes 589832 | tf_op jit(solution)/shard_map/ppermute | solution.py:23
  87.7 11.6 %collective-permute-start.10 = (bf16[1,384,256]{2,1,0:T(8,128)(2,1)S(1)}, bf16[1,384,256]{2,1,0:T(8,128)(2,1)S(1)}, u32[]{:S(2)}, u32[]{:S(2)}) collective-permute-start(bf16[1,384,256]{2,1,0:T(8,128)(2,1)S(1)} %copy-done.4), channel_id=1, source_target_pairs={{0,22},{2,20},{4,18},{6,16},{8,30},{10,28},{12,26},{14,24},{16,6},... | collective-permute-start | bytes 589832 | tf_op jit(solution)/shard_map/ppermute | solution.py:23
  93.7 8.7 %collective-permute-start.11 = (bf16[1,384,256]{2,1,0:T(8,128)(2,1)S(1)}, bf16[1,384,256]{2,1,0:T(8,128)(2,1)S(1)}, u32[]{:S(2)}, u32[]{:S(2)}) collective-permute-start(bf16[1,384,256]{2,1,0:T(8,128)(2,1)S(1)} %copy-done.3), channel_id=1, source_target_pairs={{0,24},{2,26},{4,28},{6,30},{8,16},{10,18},{12,20},{14,22},{16,8},... | collective-permute-start | bytes 589832 | tf_op jit(solution)/shard_map/ppermute | solution.py:23
  133.0 30.0 %copy-start.7 = (f32[12,512]{1,0:T(8,128)S(1)}, f32[12,512]{1,0:T(8,128)}, u32[]{:S(2)}) copy-start(f32[12,512]{1,0:T(8,128)} %custom-call) | copy-start | bytes 73732
  194.5 48.7 %copy-start.8 = (f32[12,512]{1,0:T(8,128)}, f32[12,512]{1,0:T(8,128)S(1)}, u32[]{:S(2)}) copy-start(f32[12,512]{1,0:T(8,128)S(1)} %get-tuple-element.32) | copy-start | bytes 73732
  243.2 89.0 %copy-start.9 = (f32[2048]{0:T(1024)S(1)}, f32[2048]{0:T(1024)}, u32[]{:S(2)}) copy-start(f32[2048]{0:T(1024)} %param.30) | copy-start | bytes 24580
  243.2 89.0 %copy-start.10 = (f32[2048]{0:T(1024)S(1)}, f32[2048]{0:T(1024)}, u32[]{:S(2)}) copy-start(f32[2048]{0:T(1024)} %param.31) | copy-start | bytes 24580
  243.2 88.9 %copy-start.11 = (f32[2048]{0:T(1024)S(1)}, f32[2048]{0:T(1024)}, u32[]{:S(2)}) copy-start(f32[2048]{0:T(1024)} %param.29) | copy-start | bytes 24580
  243.2 88.9 %copy-start.12 = (f32[2048]{0:T(1024)S(1)}, f32[2048]{0:T(1024)}, u32[]{:S(2)}) copy-start(f32[2048]{0:T(1024)} %param.28) | copy-start | bytes 24580
  256.2 126.5 %copy-start.2 = (f32[256,2048]{1,0:T(8,128)S(1)}, f32[256,2048]{1,0:T(8,128)}, u32[]{:S(2)}) copy-start(f32[256,2048]{1,0:T(8,128)} %param.23) | copy-start | bytes 6291460
Sparse Core Ops, SparseCore 0:
  256.3 126.2 all-reduce.2
